TPU v7x, 128 devices: a whole 4x4x4 slice. The times are simulated.
128 devices in a mesh: shard: 16 (over z, x), context: 4 (over y), tensor: 2 (over core).
Axes of the slice: x: 4, y: 4, z: 4, core: 2. Of those that a mesh axis runs over, the one named last changes fastest.
Arguments:
- inputs: float32 [32, 512, 768], P('shard', 'context'), may hold values from -6 to 6
- segment_ids: int32 [32, 512], P('shard', 'context'), may hold values from 0 to 3, never falling along the last dimension, each value on 1 to 256 neighbouring positions
- projection: bfloat16 [2, 3, 768, 768], P(None, None, 'shard', 'tensor'), may hold values from -1 to 1
- head_bias: bfloat16 [2, 2, 12, 64], P(None, None, 'tensor', 'shard'), may hold values from -3 to 3
- mixing: bfloat16 [2, 768, 768], P(None, 'tensor', 'shard'), may hold values from -0.875 to 0.875
- expansion: bfloat16 [2, 768, 3072], P(None, 'shard', 'tensor'), may hold values from -0.21875 to 0.21875
- hidden_bias: bfloat16 [2, 48, 64], P(None, 'tensor', 'shard'), may hold values from -3 to 3
- contraction: bfloat16 [2, 3072, 768], P(None, 'tensor', 'shard'), may hold values from -0.109375 to 0.109375
- norm_gains: bfloat16 [2, 2, 768], P(None, None, 'shard'), may hold values from 0.3984375 to 1.59375
- offsets: bfloat16 [2, 4, 768], P(None, None, 'shard'), may hold values from -2 to 2
- cotangent: float32 [32, 512, 768], P('shard', 'context'), may hold values from -6 to 6
Outputs:
- outputs: float32 [32, 512, 768], P('shard', 'context')
- input_grad: float32 [32, 512, 768], P('shard', 'context')
- grad_projection: float32 [2, 3, 768, 768], P(None, None, 'shard', 'tensor')
- head_grad: float32 [2, 2, 12, 64], P(None, None, 'tensor', 'shard')
- grad_mixing: float32 [2, 768, 768], P(None, 'tensor', 'shard')
- grad_expansion: float32 [2, 768, 3072], P(None, 'shard', 'tensor')
- hidden_grad: float32 [2, 48, 64], P(None, 'tensor', 'shard')
- grad_contraction: float32 [2, 3072, 768], P(None, 'tensor', 'shard')
- gains_grad: float32 [2, 2, 768], P(None, None, 'shard')
- grad_offsets: float32 [2, 4, 768], P(None, None, 'shard')
Inputs may be any that keep to these rules, and one draw needn't show every extreme that they name: `segment_ids`: within a row ids never fall; every document holds 1 to 256 positions and in every row some document holds exactly 256.
All inputs are finite; a program needn't handle non-finite values.
Results may differ from a plain program's by a relative error of at most 0.033.
Values may be sent and summed in bfloat16 or wider, within the bound.
No kernel may reach another device: no remote copies, remote signals or barrier semaphores. Data moves between devices by JAX's collectives and lax.ppermute only.
A program may use at most 128 MiB of HBM per device.

v0:
```python
import jax
import jax.numpy as jnp
from jax import lax
from jax.sharding import PartitionSpec as P

HEAD = 64
EPS = 1e-05
GELU_COEF = 0.7978845608028654
GELU_CUBE = 0.044715
MASKED = -1e30


def gelu_value(preact):
    inner_arg = GELU_COEF * (preact + GELU_CUBE * preact * preact * preact)
    return 0.5 * preact * (1.0 + jnp.tanh(inner_arg))


def gelu_slope(preact):
    inner_arg = GELU_COEF * (preact + GELU_CUBE * preact * preact * preact)
    tanh_value = jnp.tanh(inner_arg)
    return 0.5 * (1.0 + tanh_value) + 0.5 * preact * (1.0 - tanh_value * tanh_value) * GELU_COEF * (
        1.0 + 3.0 * GELU_CUBE * preact * preact
    )


def norm_forward(stream):
    center = stream - jnp.mean(stream, axis=-1, keepdims=True)
    spread = lax.rsqrt(jnp.mean(center * center, axis=-1, keepdims=True) + EPS)
    return (center * spread, spread)


def norm_backward(upstream, normed, spread, gain_row):
    scaled = upstream * gain_row
    first_mean = jnp.mean(scaled, axis=-1, keepdims=True)
    second_mean = jnp.mean(scaled * normed, axis=-1, keepdims=True)
    return spread * (scaled - first_mean - normed * second_mean)


def masked_scores(query_block, key_block, visible, head_scale):
    scores = (
        jnp.einsum("rqhe,rkhe->rhqk", query_block, key_block, preferred_element_type=jnp.float32)
        * head_scale
    )
    return jnp.where(visible, scores, MASKED)


def per_device(
    inputs,
    segment_ids,
    projection,
    head_bias,
    mixing,
    expansion,
    hidden_bias,
    contraction,
    norm_gains,
    offsets,
    cotangent,
):
    layers = projection.shape[0]
    row_count, block_length, model_width = inputs.shape
    context_size = lax.axis_size("context")
    heads_here = head_bias.shape[2]
    head_scale = HEAD ** (-0.5)
    segment_half = segment_ids.astype(jnp.bfloat16)
    query_pos = lax.axis_index("context") * block_length + jnp.arange(block_length, dtype=jnp.int32)
    key_pos = jnp.arange(block_length * context_size, dtype=jnp.int32)
    stream = inputs
    kept_state = []
    for layer_index in range(layers):
        weights = (
            lax.all_gather(projection[layer_index], "shard", axis=1, tiled=True),
            lax.all_gather(head_bias[layer_index], "shard", axis=2, tiled=True),
            lax.all_gather(mixing[layer_index], "shard", axis=1, tiled=True),
            lax.all_gather(expansion[layer_index], "shard", axis=0, tiled=True),
            lax.all_gather(hidden_bias[layer_index], "shard", axis=1, tiled=True),
            lax.all_gather(contraction[layer_index], "shard", axis=1, tiled=True),
            lax.all_gather(norm_gains[layer_index], "shard", axis=1, tiled=True),
            lax.all_gather(offsets[layer_index], "shard", axis=1, tiled=True),
        )
        (
            qkv_weight,
            qkv_bias,
            out_weight,
            up_weight,
            up_bias,
            down_weight,
            gain_rows,
            offset_rows,
        ) = weights
        gain_float = gain_rows.astype(jnp.float32)
        offset_float = offset_rows.astype(jnp.float32)
        normed_one, spread_one = norm_forward(stream)
        attend_input = (normed_one * gain_float[0] + offset_float[0]).astype(jnp.bfloat16)
        projected = jnp.einsum(
            "rtd,jdc->jrtc", attend_input, qkv_weight, preferred_element_type=jnp.float32
        )
        bias_float = qkv_bias.astype(jnp.float32).reshape(2, -1)
        query_rows = (projected[0] + bias_float[0]).astype(jnp.bfloat16)
        key_rows = projected[1].astype(jnp.bfloat16)
        value_rows = (projected[2] + bias_float[1]).astype(jnp.bfloat16)
        keys_all, values_all, segments_all = (
            lax.all_gather(key_rows, "context", axis=1, tiled=True),
            lax.all_gather(value_rows, "context", axis=1, tiled=True),
            lax.all_gather(segment_half, "context", axis=1, tiled=True),
        )
        visible = (segments_all[:, None, :] == segment_half[:, :, None]) & (
            key_pos[None, None, :] <= query_pos[None, :, None]
        )
        visible = visible[:, None]
        query_block = query_rows.reshape(row_count, block_length, heads_here, HEAD)
        key_block = keys_all.reshape(row_count, -1, heads_here, HEAD)
        value_block = values_all.reshape(row_count, -1, heads_here, HEAD)
        masked = masked_scores(query_block, key_block, visible, head_scale)
        row_top = jnp.max(masked, axis=-1, keepdims=True)
        log_total = row_top + jnp.log(jnp.sum(jnp.exp(masked - row_top), axis=-1, keepdims=True))
        soft_half = jnp.exp(masked - log_total).astype(jnp.bfloat16)
        attended = (
            jnp.einsum(
                "rhqk,rkhe->rqhe", soft_half, value_block, preferred_element_type=jnp.float32
            )
            .astype(jnp.bfloat16)
            .reshape(row_count, block_length, -1)
        )
        attend_part = jnp.einsum(
            "rtc,cd->rtd", attended, out_weight, preferred_element_type=jnp.float32
        )
        middle = stream + lax.psum(attend_part, "tensor") + offset_float[2]
        normed_two, spread_two = norm_forward(middle)
        feed_input = (normed_two * gain_float[1] + offset_float[1]).astype(jnp.bfloat16)
        preact = jnp.einsum(
            "rtd,df->rtf", feed_input, up_weight, preferred_element_type=jnp.float32
        ) + up_bias.astype(jnp.float32).reshape(-1)
        activation = gelu_value(preact).astype(jnp.bfloat16)
        feed_part = jnp.einsum(
            "rtf,fd->rtd", activation, down_weight, preferred_element_type=jnp.float32
        )
        stream = middle + lax.psum(feed_part, "tensor") + offset_float[3]
        stored = ()
        kept_state.append(
            (
                stored,
                normed_one,
                spread_one,
                attend_input,
                query_block,
                key_block,
                value_block,
                visible,
                log_total,
                attended,
                normed_two,
                spread_two,
                feed_input,
                preact,
                activation,
            )
        )
    upstream = cotangent
    collected = []
    for layer_index in reversed(range(layers)):
        (
            stored,
            normed_one,
            spread_one,
            attend_input,
            query_block,
            key_block,
            value_block,
            visible,
            log_total,
            attended,
            normed_two,
            spread_two,
            feed_input,
            preact,
            activation,
        ) = kept_state[layer_index]
        current = (
            lax.all_gather(projection[layer_index], "shard", axis=1, tiled=True),
            lax.all_gather(head_bias[layer_index], "shard", axis=2, tiled=True),
            lax.all_gather(mixing[layer_index], "shard", axis=1, tiled=True),
            lax.all_gather(expansion[layer_index], "shard", axis=0, tiled=True),
            lax.all_gather(hidden_bias[layer_index], "shard", axis=1, tiled=True),
            lax.all_gather(contraction[layer_index], "shard", axis=1, tiled=True),
            lax.all_gather(norm_gains[layer_index], "shard", axis=1, tiled=True),
            lax.all_gather(offsets[layer_index], "shard", axis=1, tiled=True),
        )
        (
            qkv_weight,
            qkv_bias,
            out_weight,
            up_weight,
            up_bias,
            down_weight,
            gain_rows,
            offset_rows,
        ) = current
        gain_float = gain_rows.astype(jnp.float32)
        upstream_half = upstream.astype(jnp.bfloat16)
        contraction_part = jnp.einsum(
            "rtf,rtd->fd", activation, upstream_half, preferred_element_type=jnp.float32
        )
        offset_down = jnp.sum(upstream, axis=(0, 1))
        hidden_back = jnp.einsum(
            "rtd,fd->rtf", upstream_half, down_weight, preferred_element_type=jnp.float32
        ) * gelu_slope(preact)
        hidden_half = hidden_back.astype(jnp.bfloat16)
        hidden_part = jnp.sum(hidden_back, axis=(0, 1)).reshape(up_bias.shape)
        expansion_part = jnp.einsum(
            "rtd,rtf->df", feed_input, hidden_half, preferred_element_type=jnp.float32
        )
        feed_partial = jnp.einsum(
            "rtf,df->rtd", hidden_half, up_weight, preferred_element_type=jnp.float32
        )
        feed_back = lax.psum(feed_partial.astype(jnp.bfloat16), "tensor").astype(jnp.float32)
        gain_two = jnp.sum(feed_back * normed_two, axis=(0, 1))
        offset_two = jnp.sum(feed_back, axis=(0, 1))
        middle_back = upstream + norm_backward(feed_back, normed_two, spread_two, gain_float[1])
        middle_half = middle_back.astype(jnp.bfloat16)
        mixing_part = jnp.einsum(
            "rtc,rtd->cd", attended, middle_half, preferred_element_type=jnp.float32
        )
        offset_mix = jnp.sum(middle_back, axis=(0, 1))
        attended_back = jnp.einsum(
            "rtd,cd->rtc", middle_half, out_weight, preferred_element_type=jnp.float32
        ).astype(jnp.bfloat16)
        back_heads = attended_back.reshape(row_count, block_length, heads_here, HEAD)
        attended_heads = attended.reshape(row_count, block_length, heads_here, HEAD)
        row_delta = jnp.sum(
            back_heads.astype(jnp.float32) * attended_heads.astype(jnp.float32), axis=-1
        )
        masked = masked_scores(query_block, key_block, visible, head_scale)
        soft = jnp.exp(masked - log_total)
        soft_half = soft.astype(jnp.bfloat16)
        prob_back = jnp.einsum(
            "rqhe,rkhe->rhqk", back_heads, value_block, preferred_element_type=jnp.float32
        )
        score_back = (
            soft * (prob_back - jnp.transpose(row_delta, (0, 2, 1))[..., None]) * head_scale
        ).astype(jnp.bfloat16)
        query_back = jnp.einsum(
            "rhqk,rkhe->rqhe", score_back, key_block, preferred_element_type=jnp.float32
        ).reshape(row_count, block_length, -1)
        key_full = jnp.einsum(
            "rhqk,rqhe->rkhe", score_back, query_block, preferred_element_type=jnp.float32
        ).reshape(row_count, block_length * context_size, -1)
        value_full = jnp.einsum(
            "rhqk,rqhe->rkhe", soft_half, back_heads, preferred_element_type=jnp.float32
        ).reshape(row_count, block_length * context_size, -1)
        key_back, value_back = (
            lax.psum_scatter(
                key_full.astype(jnp.bfloat16), "context", scatter_dimension=1, tiled=True
            ).astype(jnp.float32),
            lax.psum_scatter(
                value_full.astype(jnp.bfloat16), "context", scatter_dimension=1, tiled=True
            ).astype(jnp.float32),
        )
        head_part = jnp.stack(
            [jnp.sum(query_back, axis=(0, 1)), jnp.sum(value_back, axis=(0, 1))]
        ).reshape(qkv_bias.shape)
        project_back = jnp.stack([query_back, key_back, value_back]).astype(jnp.bfloat16)
        projection_part = jnp.einsum(
            "rtd,jrtc->jdc", attend_input, project_back, preferred_element_type=jnp.float32
        )
        input_partial = jnp.einsum(
            "jrtc,jdc->rtd", project_back, qkv_weight, preferred_element_type=jnp.float32
        )
        input_back = lax.psum(input_partial.astype(jnp.bfloat16), "tensor").astype(jnp.float32)
        gain_one = jnp.sum(input_back * normed_one, axis=(0, 1))
        offset_one = jnp.sum(input_back, axis=(0, 1))
        upstream = middle_back + norm_backward(input_back, normed_one, spread_one, gain_float[0])
        grad_parts = (
            projection_part,
            head_part,
            mixing_part,
            expansion_part,
            hidden_part,
            contraction_part,
            jnp.stack([gain_one, gain_two]),
            jnp.stack([offset_one, offset_two, offset_mix, offset_down]),
        )
        collected.insert(
            0,
            (
                lax.psum(
                    lax.psum_scatter(
                        grad_parts[0].astype(jnp.bfloat16), "shard", scatter_dimension=1, tiled=True
                    ),
                    "context",
                ).astype(jnp.float32),
                lax.psum(
                    lax.psum_scatter(
                        grad_parts[1].astype(jnp.bfloat16), "shard", scatter_dimension=2, tiled=True
                    ),
                    "context",
                ).astype(jnp.float32),
                lax.psum(
                    lax.psum_scatter(
                        grad_parts[2].astype(jnp.bfloat16), "shard", scatter_dimension=1, tiled=True
                    ),
                    "context",
                ).astype(jnp.float32),
                lax.psum(
                    lax.psum_scatter(
                        grad_parts[3].astype(jnp.bfloat16), "shard", scatter_dimension=0, tiled=True
                    ),
                    "context",
                ).astype(jnp.float32),
                lax.psum(
                    lax.psum_scatter(
                        grad_parts[4].astype(jnp.bfloat16), "shard", scatter_dimension=1, tiled=True
                    ),
                    "context",
                ).astype(jnp.float32),
                lax.psum(
                    lax.psum_scatter(
                        grad_parts[5].astype(jnp.bfloat16), "shard", scatter_dimension=1, tiled=True
                    ),
                    "context",
                ).astype(jnp.float32),
                lax.psum(
                    lax.psum_scatter(
                        grad_parts[6].astype(jnp.bfloat16), "shard", scatter_dimension=1, tiled=True
                    ),
                    "context",
                ).astype(jnp.float32),
                lax.psum(
                    lax.psum_scatter(
                        grad_parts[7].astype(jnp.bfloat16), "shard", scatter_dimension=1, tiled=True
                    ),
                    "context",
                ).astype(jnp.float32),
            ),
        )
    stacked = [jnp.stack([entry[member] for entry in collected]) for member in range(8)]
    return (
        stream,
        upstream,
        stacked[0],
        stacked[1],
        stacked[2],
        stacked[3],
        stacked[4],
        stacked[5],
        stacked[6],
        stacked[7],
    )


def solution(mesh):
    in_specs = (
        P("shard", "context", None),
        P("shard", "context"),
        P(None, None, "shard", "tensor"),
        P(None, None, "tensor", "shard"),
        P(None, "tensor", "shard"),
        P(None, "shard", "tensor"),
        P(None, "tensor", "shard"),
        P(None, "tensor", "shard"),
        P(None, None, "shard"),
        P(None, None, "shard"),
        P("shard", "context", None),
    )
    out_specs = (
        P("shard", "context", None),
        P("shard", "context", None),
        P(None, None, "shard", "tensor"),
        P(None, None, "tensor", "shard"),
        P(None, "tensor", "shard"),
        P(None, "shard", "tensor"),
        P(None, "tensor", "shard"),
        P(None, "tensor", "shard"),
        P(None, None, "shard"),
        P(None, None, "shard"),
    )
    return jax.shard_map(
        per_device, mesh=mesh, in_specs=in_specs, out_specs=out_specs, check_vma=False
    )
```

profile of v0, /device:TPU:0, one launch (start us, length us, event | category | flops | bytes accessed | tf_op | source)
XLA Modules:
  0.0 1538.7 jit_solution(7133893320823804238)
XLA Ops:
  10.4 25.5 %all-gather.1 = bf16[1,4,768]{1,0,2:T(2,128)(2,1)S(1)} all-gather(bf16[1,4,48]{1,0,2:T(2,128)(2,1)S(1)} %copy.288), channel_id=3, replica_groups=mesh['shard'=16,'context'=4,'tensor'=2] {'shard'}, dimensions={2}, use_global_device_ids=true | all-gather | bytes 6528 | tf_op jit(solution)/shard_map/all_gather | solution.py:79
  37.0 23.4 %all-gather = bf16[1,2,768]{1,0,2:T(2,128)(2,1)S(1)} all-gather(bf16[1,2,48]{1,0,2:T(2,128)(2,1)S(1)} %copy.287), channel_id=2, replica_groups=mesh['shard'=16,'context'=4,'tensor'=2] {'shard'}, dimensions={2}, use_global_device_ids=true | all-gather | bytes 3264 | tf_op jit(solution)/shard_map/all_gather | solution.py:78
  61.4 21.3 %all-gather.3 = bf16[1,2,6,64]{2,1,0,3:T(2,128)(2,1)S(1)} all-gather(bf16[1,2,6,4]{2,1,0,3:T(2,128)(2,1)S(1)} %copy.289), channel_id=5, replica_groups=mesh['shard'=16,'context'=4,'tensor'=2] {'shard'}, dimensions={3}, use_global_device_ids=true | all-gather | bytes 1632 | tf_op jit(solution)/shard_map/all_gather | solution.py:73
  83.1 10.0 all_gather.79
  93.1 23.9 %all-gather.5 = bf16[1,384,768]{1,2,0:T(8,128)(2,1)S(1)} all-gather(bf16[1,384,48]{1,2,0:T(8,128)(2,1)S(1)} %get-tuple-element.105), channel_id=7, replica_groups=mesh['shard'=16,'context'=4,'tensor'=2] {'shard'}, dimensions={2}, use_global_device_ids=true | all-gather | bytes 626688 | tf_op jit(solution)/shard_map/all_gather | solution.py:74
  117.2 4.6 slice_reduce_fusion.8
  122.1 11.0 slice_reduce_fusion.6
  136.3 14.4 all-gather.4
  157.9 13.3 all_gather.78
  171.6 3.1 convolution_convert_fusion.5
  178.3 21.3 %all-gather.7 = bf16[1,24,64]{1,0,2:T(2,128)(2,1)S(1)} all-gather(bf16[1,24,4]{1,0,2:T(2,128)(2,1)S(1)} %copy.290), channel_id=9, replica_groups=mesh['shard'=16,'context'=4,'tensor'=2] {'shard'}, dimensions={2}, use_global_device_ids=true | all-gather | bytes 3264 | tf_op jit(solution)/shard_map/all_gather | solution.py:76
  201.3 47.0 %all-gather.27.cloned.1.call-done = bf16[1,768,1536]{2,1,0:T(8,128)(2,1)} async-done(((bf16[1,48,1536]{2,1,0:T(8,128)(2,1)}), bf16[1,768,1536]{2,1,0:T(8,128)(2,1)}) %all-gather.27.cloned.1.call-update) | async-done | bytes 2359312 | tf_op jit(solution)/shard_map/all_gather | solution.py:75
  248.4 2.5 convolution_add_fusion.1
  250.9 45.3 %all-gather.29.cloned.1.call-done = bf16[1,1536,768]{1,2,0:T(8,128)(2,1)} async-done(((bf16[1,1536,48]{1,2,0:T(8,128)(2,1)}), bf16[1,1536,768]{1,2,0:T(8,128)(2,1)}) %all-gather.29.cloned.1.call-update) | async-done | bytes 2359312 | tf_op jit(solution)/shard_map/all_gather | solution.py:77
  296.2 3.6 fusion.6
  300.7 23.3 %all-gather.10 = bf16[1,4,768]{1,0,2:T(2,128)(2,1)S(1)} all-gather(bf16[1,4,48]{1,0,2:T(2,128)(2,1)S(1)} %copy.292), channel_id=12, replica_groups=mesh['shard'=16,'context'=4,'tensor'=2] {'shard'}, dimensions={2}, use_global_device_ids=true | all-gather | bytes 6528 | tf_op jit(solution)/shard_map/all_gather | solution.py:79
  324.5 22.4 %all-gather.9 = bf16[1,2,768]{1,0,2:T(2,128)(2,1)S(1)} all-gather(bf16[1,2,48]{1,0,2:T(2,128)(2,1)S(1)} %copy.291), channel_id=11, replica_groups=mesh['shard'=16,'context'=4,'tensor'=2] {'shard'}, dimensions={2}, use_global_device_ids=true | all-gather | bytes 3264 | tf_op jit(solution)/shard_map/all_gather | solution.py:78
  347.3 22.1 %all-gather.12 = bf16[1,2,6,64]{2,1,0,3:T(2,128)(2,1)S(1)} all-gather(bf16[1,2,6,4]{2,1,0,3:T(2,128)(2,1)S(1)} %copy.293), channel_id=14, replica_groups=mesh['shard'=16,'context'=4,'tensor'=2] {'shard'}, dimensions={3}, use_global_device_ids=true | all-gather | bytes 1632 | tf_op jit(solution)/shard_map/all_gather | solution.py:73
  370.8 24.5 %all-gather.14 = bf16[1,384,768]{1,2,0:T(8,128)(2,1)} all-gather(bf16[1,384,48]{1,2,0:T(8,128)(2,1)S(1)} %get-tuple-element.104), channel_id=16, replica_groups=mesh['shard'=16,'context'=4,'tensor'=2] {'shard'}, dimensions={2}, use_global_device_ids=true | all-gather | bytes 626688 | tf_op jit(solution)/shard_map/all_gather | solution.py:74
  395.4 4.6 slice_reduce_fusion.2
  400.0 11.2 slice_reduce_fusion
  416.2 15.3 all-gather.13
  438.4 14.1 all_gather.89
  454.7 3.1 convolution_convert_fusion.4
  460.8 22.6 %all-gather.16 = bf16[1,24,64]{1,0,2:T(2,128)(2,1)S(1)} all-gather(bf16[1,24,4]{1,0,2:T(2,128)(2,1)S(1)} %copy.294), channel_id=18, replica_groups=mesh['shard'=16,'context'=4,'tensor'=2] {'shard'}, dimensions={2}, use_global_device_ids=true | all-gather | bytes 3264 | tf_op jit(solution)/shard_map/all_gather | solution.py:76
  486.8 44.9 %all-gather.33.cloned.1.call-done = bf16[1,768,1536]{2,1,0:T(8,128)(2,1)} async-done(((bf16[1,48,1536]{2,1,0:T(8,128)(2,1)}), bf16[1,768,1536]{2,1,0:T(8,128)(2,1)}) %all-gather.33.cloned.1.call-update) | async-done | bytes 2359312 | tf_op jit(solution)/shard_map/all_gather | solution.py:75
  531.7 3.7 convolution_add_fusion
  535.4 43.8 %all-gather.35.cloned.1.call-done = bf16[1,1536,768]{1,2,0:T(8,128)(2,1)} async-done(((bf16[1,1536,48]{1,2,0:T(8,128)(2,1)}), bf16[1,1536,768]{1,2,0:T(8,128)(2,1)}) %all-gather.35.cloned.1.call-update) | async-done | bytes 2359312 | tf_op jit(solution)/shard_map/all_gather | solution.py:77
  579.1 4.5 fusion.157
  586.1 4.1 fusion.3
  590.5 19.0 %all-reduce.36.cloned.1.call-done = bf16[2,128,768]{2,1,0:T(8,128)(2,1)} async-done(((bf16[2,128,768]{2,1,0:T(8,128)(2,1)}), bf16[2,128,768]{2,1,0:T(8,128)(2,1)}) %all-reduce.36.cloned.1.call-update) | async-done | bytes 393232 | tf_op jit(solution)/shard_map/psum | solution.py:216
  612.0 26.7 %all-reduce.34.cloned.1.call-done = f32[2,128,768]{2,1,0:T(8,128)} async-done(((f32[2,128,768]{2,1,0:T(8,128)}), f32[2,128,768]{2,1,0:T(8,128)}) %all-reduce.34.cloned.1.call-update) | async-done | bytes 786448 | tf_op jit(solution)/shard_map/psum | solution.py:138
  638.7 3.4 fusion.140
  646.9 3.5 multiply_convert_fusion.1
  652.8 2.4 copy.234
  655.3 3.8 convolution_convert_fusion.2
  661.5 2.4 fusion.146
  664.7 14.6 reduce-scatter.21.cloned.1.call-done
  679.2 24.7 %reduce-scatter.23.cloned.1.call-done = bf16[2,128,384]{2,1,0:T(8,128)(2,1)} async-done(((bf16[2,512,384]{2,1,0:T(8,128)(2,1)}), bf16[2,128,384]{2,1,0:T(8,128)(2,1)}) %reduce-scatter.23.cloned.1.call-update) | async-done | bytes 196624 | tf_op jit(solution)/shard_map/reduce_scatter | solution.py:255
  704.0 3.3 fusion.50
  707.3 24.0 %all-reduce.38.cloned.1.call-done = bf16[2,128,768]{2,1,0:T(8,128)(2,1)} async-done(((bf16[2,128,768]{2,1,0:T(8,128)(2,1)}), bf16[2,128,768]{2,1,0:T(8,128)(2,1)}) %all-reduce.38.cloned.1.call-update) | async-done | bytes 393232 | tf_op jit(solution)/shard_map/psum | solution.py:269
  738.9 25.5 %all-reduce.40.cloned.1.call-done = bf16[2,128,768]{2,1,0:T(8,128)(2,1)} async-done(((bf16[2,128,768]{2,1,0:T(8,128)(2,1)}), bf16[2,128,768]{2,1,0:T(8,128)(2,1)}) %all-reduce.40.cloned.1.call-update) | async-done | bytes 393232 | tf_op jit(solution)/shard_map/psum | solution.py:216
  772.2 3.5 multiply_convert_fusion
  780.8 3.9 convolution_convert_fusion
  787.0 3.0 fusion.145
  791.8 12.8 reduce-scatter.25.cloned.1.call-done
  804.6 24.5 %reduce-scatter.27.cloned.1.call-done = bf16[2,128,384]{2,1,0:T(8,128)(2,1)} async-done(((bf16[2,512,384]{2,1,0:T(8,128)(2,1)}), bf16[2,128,384]{2,1,0:T(8,128)(2,1)}) %reduce-scatter.27.cloned.1.call-update) | async-done | bytes 196624 | tf_op jit(solution)/shard_map/reduce_scatter | solution.py:255
  829.1 3.2 fusion.53
  832.4 2.5 fusion.43
  837.4 3.1 fusion.35
  840.5 5.3 copy.244
  847.9 5.2 copy.242
  857.7 3.9 bitcast_convert_fusion
  862.7 2.4 bitcast_convert_fusion.3
  866.7 2.4 bitcast_convert_fusion.1
  875.5 75.6 %all-reduce.12 = (bf16[2,6,64]{1,0,2:T(2,128)(2,1)S(1)}, bf16[2,6,64]{1,0,2:T(2,128)(2,1)S(1)}, bf16[24,64]{1,0:T(8,128)(2,1)S(1)}, bf16[24,64]{1,0:T(8,128)(2,1...) all-reduce(bf16[2,6,64]{1,0,2:T(2,128)(2,1)S(1)} %copy.249, ...), channel_id=27, replica_groups=mesh['shard'=16,'context'=4,'tensor'=2] {'shard'}, use_global_device_ids=true, to_apply=%region_44.45.clone | all-reduce | flops 13824 | bytes 55296
  956.3 52.0 %reduce-scatter.37.cloned.1.call-done = bf16[384,48]{0,1:T(8,128)(2,1)} async-done(((bf16[384,768]{0,1:T(8,128)(2,1)}), bf16[384,48]{0,1:T(8,128)(2,1)}) %reduce-scatter.37.cloned.1.call-update) | async-done | bytes 36880
  1008.4 111.1 %all-reduce.44.cloned.1.call-done = (bf16[3,768,384]{2,0,1:T(4,128)(2,1)}, bf16[3,768,384]{2,0,1:T(4,128)(2,1)}) async-done(((bf16[3,768,384]{2,0,1:T(4,128)(2,1)}, bf16[3,768,384]{2,0,1:T(4,128)(2,1)}), (bf16[3,768,384]{2,0,1:T(4,128)(2,1)}, bf16[3,768,384]{2,0,1:T(4,128)(2,1)})) %all-reduce.44.cloned.1.call-update) | async-done | bytes 3538960
  1122.7 75.1 %reduce-scatter.31.cloned.1.call-done = bf16[48,1536]{1,0:T(8,128)(2,1)} async-done(((bf16[768,1536]{1,0:T(8,128)(2,1)}), bf16[48,1536]{1,0:T(8,128)(2,1)}) %reduce-scatter.31.cloned.1.call-update) | async-done | bytes 147472 | tf_op jit(solution)/shard_map/reduce_scatter | solution.py:305
  1197.8 77.9 %reduce-scatter.35.cloned.1.call-done = bf16[1536,48]{0,1:T(8,128)(2,1)} async-done(((bf16[1536,768]{0,1:T(8,128)(2,1)}), bf16[1536,48]{0,1:T(8,128)(2,1)}) %reduce-scatter.35.cloned.1.call-update) | async-done | bytes 147472 | tf_op jit(solution)/shard_map/reduce_scatter | solution.py:317
  1275.7 77.7 %reduce-scatter.29.cloned.1.call-done = bf16[48,1536]{1,0:T(8,128)(2,1)} async-done(((bf16[768,1536]{1,0:T(8,128)(2,1)}), bf16[48,1536]{1,0:T(8,128)(2,1)}) %reduce-scatter.29.cloned.1.call-update) | async-done | bytes 147472 | tf_op jit(solution)/shard_map/reduce_scatter | solution.py:305
  1353.3 77.9 %reduce-scatter.33.cloned.1.call-done = bf16[1536,48]{0,1:T(8,128)(2,1)} async-done(((bf16[1536,768]{0,1:T(8,128)(2,1)}), bf16[1536,48]{0,1:T(8,128)(2,1)}) %reduce-scatter.33.cloned.1.call-update) | async-done | bytes 147472 | tf_op jit(solution)/shard_map/reduce_scatter | solution.py:317
  1432.5 43.3 %all-reduce.46.cloned.1.call-done = (bf16[1,2,6,4]{2,3,1,0:T(4,128)(2,1)}, bf16[1,2,6,4]{2,3,1,0:T(4,128)(2,1)}, bf16[1,384,48]{1,2,0:T(8,128)(2,1)}, bf16[1,384...) async-done(((bf16[1,2,6,4]{2,3,1,0:T(4,128)(2,1)}, ...) | async-done | bytes 75472 | tf_op jit(solution)/shard_map/psum | solution.py:292
  1482.4 42.9 %all-reduce.48.cloned.1.call-done = (bf16[1,3,48,384]{3,1,2,0:T(4,128)(2,1)}, bf16[1,3,48,384]{3,1,2,0:T(4,128)(2,1)}, bf16[1,48,1536]{2,1,0:T(8,128)(2,1)}, bf1...) async-done(((bf16[1,3,48,384]{3,1,2,0:T(4,128)(2,1)}, bf16[1,3,48,384]{3,1,2,0:T(4,128)(2,1)}, bf16[1,48,1536]{2,1,0:T(8,128)(2,1)}, ...) | async-done | bytes 811024 | tf_op jit(solution)/shard_map/psum | solution.py:286
  (409 shorter events, 124.9 us)
Async XLA Ops:
  7.2 29.1 %copy-start.83 = (bf16[2,2,48]{2,1,0:T(2,128)(2,1)S(1)}, bf16[2,2,48]{2,1,0:T(2,128)(2,1)}, u32[]{:S(2)}) copy-start(bf16[2,2,48]{2,1,0:T(2,128)(2,1)} %param.19) | copy-start | bytes 1156
  7.2 53.6 %copy-start.88 = (s32[2,128]{1,0:T(2,128)S(1)}, s32[2,128]{1,0:T(2,128)}, u32[]{:S(2)}) copy-start(s32[2,128]{1,0:T(2,128)} %param.12) | copy-start | bytes 3076
  7.2 53.6 %copy-start.76 = (bf16[2,2,6,4]{2,3,1,0:T(4,128)(2,1)S(1)}, bf16[2,2,6,4]{2,3,1,0:T(4,128)(2,1)}, u32[]{:S(2)}) copy-start(bf16[2,2,6,4]{2,3,1,0:T(4,128)(2,1)} %param.14) | copy-start | bytes 580
  7.2 75.7 %copy-start = (f32[2,128,768]{2,1,0:T(8,128)S(1)}, f32[2,128,768]{2,1,0:T(8,128)}, u32[]{:S(2)}) copy-start(f32[2,128,768]{2,1,0:T(8,128)} %param.11) | copy-start | bytes 2359300
  7.2 126.0 %all-gather.25.cloned.1.call-start = ((), (), s32[]{:S(2)}) async-start(), calls=%async_computation.26 | async-start | bytes 1880064 | tf_op jit(solution)/shard_map/all_gather | solution.py:72
  9.0 84.1 %copy-start.41 = (bf16[2,384,48]{1,2,0:T(8,128)(2,1)S(1)}, bf16[2,384,48]{1,2,0:T(8,128)(2,1)}, u32[]{:S(2)}) copy-start(bf16[2,384,48]{1,2,0:T(8,128)(2,1)} %param.15) | copy-start | bytes 221188
  9.0 190.7 %all-reduce.28.cloned.1.call-start = ((), (), s32[]{:S(2)}) async-start(), calls=%async_computation.10 | async-start | bytes 1572864 | tf_op jit(solution)/shard_map/psum | solution.py:128
  82.8 71.6 %copy-start.50 = (f32[6,64]{1,0:T(8,128)}, f32[6,64]{1,0:T(8,128)S(1)}, u32[]{:S(2)}) copy-start(f32[6,64]{1,0:T(8,128)S(1)} %copy.213) | copy-start | bytes 4612
  117.0 57.7 %copy-start.10 = (bf16[1,384,768]{1,2,0:T(8,128)(2,1)}, bf16[1,384,768]{1,2,0:T(8,128)(2,1)S(1)}, u32[]{:S(2)}) copy-start(bf16[1,384,768]{1,2,0:T(8,128)(2,1)S(1)} %all-gather.5) | copy-start | bytes 1769476
  117.0 18.5 %copy-start.46 = (f32[2,128]{1,0:T(2,128)}, f32[2,128]{1,0:T(2,128)S(1)}, u32[]{:S(2)}) copy-start(f32[2,128]{1,0:T(2,128)S(1)} %broadcast_multiply_fusion.11) | copy-start | bytes 3076
  121.8 13.7 copy-start.53
  122.1 49.4 %copy-start.20 = (pred[2,128,512]{2,1,0:T(8,128)(4,1)}, pred[2,128,512]{2,1,0:T(8,128)(4,1)S(1)}, u32[]{:S(2)}) copy-start(pred[2,128,512]{2,1,0:T(8,128)(4,1)S(1)} %compare_and_fusion) | copy-start | bytes 393220
  133.2 115.2 %copy-start.61 = (f32[768]{0:T(1024)}, f32[768]{0:T(1024)S(1)}, u32[]{:S(2)}) copy-start(f32[768]{0:T(1024)S(1)} %get-tuple-element.49) | copy-start | bytes 9220
  157.9 13.7 copy-start.71
  176.1 72.3 %all-gather.27.cloned.1.call-start = ((), (), s32[]{:S(2)}) async-start(), calls=%async_computation.27 | async-start | bytes 2506752 | tf_op jit(solution)/shard_map/all_gather | solution.py:75
  176.9 119.4 %all-gather.29.cloned.1.call-start = ((), (), s32[]{:S(2)}) async-start(), calls=%async_computation.28 | async-start | bytes 2506752 | tf_op jit(solution)/shard_map/all_gather | solution.py:77
  177.7 233.5 %all-reduce.30.cloned.1.call-start = ((), (), s32[]{:S(2)}) async-start(), calls=%async_computation.11 | async-start | bytes 1572864 | tf_op jit(solution)/shard_map/psum | solution.py:138
  201.1 49.8 %copy-start.55 = (f32[2,128]{1,0:T(2,128)}, f32[2,128]{1,0:T(2,128)S(1)}, u32[]{:S(2)}) copy-start(f32[2,128]{1,0:T(2,128)S(1)} %broadcast_multiply_fusion.10) | copy-start | bytes 3076
  201.3 49.6 %copy-start.64 = (f32[2,128]{1,0:T(2,128)}, f32[2,128]{1,0:T(2,128)S(1)}, u32[]{:S(2)}) copy-start(f32[2,128]{1,0:T(2,128)S(1)} %add_rsqrt_fusion.2) | copy-start | bytes 3076
  250.9 45.3 %copy-start.90 = (f32[2,128,1536]{2,1,0:T(8,128)}, f32[2,128,1536]{2,1,0:T(8,128)S(1)}, u32[]{:S(2)}) copy-start(f32[2,128,1536]{2,1,0:T(8,128)S(1)} %convolution_add_fusion.1) | copy-start | bytes 4718596
  250.9 49.6 %copy-start.79 = (bf16[1,4,48]{2,1,0:T(4,128)(2,1)S(1)}, bf16[1,4,48]{2,1,0:T(4,128)(2,1)}, u32[]{:S(2)}) copy-start(bf16[1,4,48]{2,1,0:T(4,128)(2,1)} %get-tuple-element.115) | copy-start | bytes 1156
  299.9 24.5 %copy-start.82 = (bf16[1,2,48]{2,1,0:T(2,128)(2,1)S(1)}, bf16[1,2,48]{2,1,0:T(2,128)(2,1)}, u32[]{:S(2)}) copy-start(bf16[1,2,48]{2,1,0:T(2,128)(2,1)} %get-tuple-element.116) | copy-start | bytes 580
  299.9 47.4 %copy-start.75 = (bf16[1,2,6,4]{2,3,1,0:T(4,128)(2,1)S(1)}, bf16[1,2,6,4]{2,3,1,0:T(4,128)(2,1)}, u32[]{:S(2)}) copy-start(bf16[1,2,6,4]{2,3,1,0:T(4,128)(2,1)} %get-tuple-element.110) | copy-start | bytes 292
  299.9 112.8 %all-gather.31.cloned.1.call-start = ((), (), s32[]{:S(2)}) async-start(), calls=%async_computation.29 | async-start | bytes 1880064 | tf_op jit(solution)/shard_map/all_gather | solution.py:72
  300.5 183.7 %all-reduce.32.cloned.1.call-start = ((), (), s32[]{:S(2)}) async-start(), calls=%async_computation.12 | async-start | bytes 1572864 | tf_op jit(solution)/shard_map/psum | solution.py:128
  437.2 17.6 %copy-start.22 = (pred[2,128,512]{2,1,0:T(8,128)(4,1)S(1)}, pred[2,128,512]{2,1,0:T(8,128)(4,1)}, u32[]{:S(2)}) copy-start(pred[2,128,512]{2,1,0:T(8,128)(4,1)} %copy-done.20) | copy-start | bytes 393220
  437.2 20.7 %copy-start.73 = (f32[2,6,128]{2,1,0:T(8,128)}, f32[2,6,128]{2,1,0:T(8,128)S(1)}, u32[]{:S(2)}) copy-start(f32[2,6,128]{2,1,0:T(8,128)S(1)} %log_add_fusion) | copy-start | bytes 18436
  457.9 26.3 %copy-start.28 = (bf16[2,6,64,128]{3,2,1,0:T(8,128)(2,1)}, bf16[2,6,64,128]{3,2,1,0:T(8,128)(2,1)S(1)}, u32[]{:S(2)}) copy-start(bf16[2,6,64,128]{3,2,1,0:T(8,128)(2,1)S(1)} %convolution_convert_fusion.4) | copy-start | bytes 589828
  459.3 72.4 %all-gather.33.cloned.1.call-start = ((), (), s32[]{:S(2)}) async-start(), calls=%async_computation.30 | async-start | bytes 2506752 | tf_op jit(solution)/shard_map/all_gather | solution.py:75
  460.0 119.1 %all-gather.35.cloned.1.call-start = ((), (), s32[]{:S(2)}) async-start(), calls=%async_computation.31 | async-start | bytes 2506752 | tf_op jit(solution)/shard_map/all_gather | solution.py:77
  460.7 148.8 %all-reduce.36.cloned.1.call-start = ((), (), s32[]{:S(2)}) async-start(), calls=%async_computation.14 | async-start | bytes 786432 | tf_op jit(solution)/shard_map/psum | solution.py:216
  579.1 5.3 copy-start.86
  586.1 52.6 %all-reduce.34.cloned.1.call-start = ((), (), s32[]{:S(2)}) async-start(), calls=%async_computation.13 | async-start | bytes 1572864 | tf_op jit(solution)/shard_map/psum | solution.py:138
  590.2 89.0 %reduce-scatter.21.cloned.1.call-start = ((), (), s32[]{:S(2)}) async-start(), calls=%async_computation.15 | async-start | bytes 983040 | tf_op jit(solution)/shard_map/reduce_scatter | solution.py:252
  655.2 48.7 %reduce-scatter.23.cloned.1.call-start = ((), (), s32[]{:S(2)}) async-start(), calls=%async_computation.16 | async-start | bytes 983040 | tf_op jit(solution)/shard_map/reduce_scatter | solution.py:255
  661.4 69.9 %all-reduce.38.cloned.1.call-start = ((), (), s32[]{:S(2)}) async-start(), calls=%async_computation.17 | async-start | bytes 786432 | tf_op jit(solution)/shard_map/psum | solution.py:269
  704.0 27.3 %copy-start.49 = (f32[2,128]{1,0:T(2,128)S(1)}, f32[2,128]{1,0:T(2,128)}, u32[]{:S(2)}) copy-start(f32[2,128]{1,0:T(2,128)} %copy-done.48) | copy-start | bytes 3076
  704.0 27.3 %copy-start.58 = (f32[2,128]{1,0:T(2,128)S(1)}, f32[2,128]{1,0:T(2,128)}, u32[]{:S(2)}) copy-start(f32[2,128]{1,0:T(2,128)} %copy-done.57) | copy-start | bytes 3076
  707.2 57.2 %all-reduce.40.cloned.1.call-start = ((), (), s32[]{:S(2)}) async-start(), calls=%async_computation.18 | async-start | bytes 786432 | tf_op jit(solution)/shard_map/psum | solution.py:216
  737.3 27.1 %copy-start.56 = (f32[2,128]{1,0:T(2,128)S(1)}, f32[2,128]{1,0:T(2,128)}, u32[]{:S(2)}) copy-start(f32[2,128]{1,0:T(2,128)} %copy-done.55) | copy-start | bytes 3076
  737.3 27.1 %copy-start.65 = (f32[2,128]{1,0:T(2,128)S(1)}, f32[2,128]{1,0:T(2,128)}, u32[]{:S(2)}) copy-start(f32[2,128]{1,0:T(2,128)} %copy-done.64) | copy-start | bytes 3076
  738.9 65.7 %reduce-scatter.25.cloned.1.call-start = ((), (), s32[]{:S(2)}) async-start(), calls=%async_computation.19 | async-start | bytes 983040 | tf_op jit(solution)/shard_map/reduce_scatter | solution.py:252
  765.9 5.3 copy-start.27
  772.2 4.7 copy-start.18
  772.2 4.7 copy-start.51
  780.5 48.5 %reduce-scatter.27.cloned.1.call-start = ((), (), s32[]{:S(2)}) async-start(), calls=%async_computation.20 | async-start | bytes 983040 | tf_op jit(solution)/shard_map/reduce_scatter | solution.py:255
  787.0 85.9 %all-reduce.42.cloned.1.call-start = ((), (), s32[]{:S(2)}) async-start(), calls=%async_computation.21 | async-start | bytes 786432 | tf_op jit(solution)/shard_map/psum | solution.py:269
  832.3 123.9 %reduce-scatter.39.cloned.1.call-start = ((), (), s32[]{:S(2)}) async-start(), calls=%async_computation.33 | async-start | bytes 626688
  834.9 173.4 %reduce-scatter.37.cloned.1.call-start = ((), (), s32[]{:S(2)}) async-start(), calls=%async_computation.32 | async-start | bytes 626688
  837.3 282.1 %all-reduce.44.cloned.1.call-start = ((), (), s32[]{:S(2)}) async-start(), calls=%async_computation.34 | async-start | bytes 9437184
  840.5 5.3 copy-start.39
  840.5 5.3 copy-start.40
  840.5 5.3 copy-start.43
  840.5 5.3 copy-start.47
  840.5 5.3 copy-start.54
  840.5 5.3 copy-start.87
  853.1 344.7 %reduce-scatter.31.cloned.1.call-start = ((), (), s32[]{:S(2)}) async-start(), calls=%async_computation.23 | async-start | bytes 2506752 | tf_op jit(solution)/shard_map/reduce_scatter | solution.py:305
  856.6 419.0 %reduce-scatter.35.cloned.1.call-start = ((), (), s32[]{:S(2)}) async-start(), calls=%async_computation.25 | async-start | bytes 2506752 | tf_op jit(solution)/shard_map/reduce_scatter | solution.py:317
  861.6 491.7 %reduce-scatter.29.cloned.1.call-start = ((), (), s32[]{:S(2)}) async-start(), calls=%async_computation.22 | async-start | bytes 2506752 | tf_op jit(solution)/shard_map/reduce_scatter | solution.py:305
  865.1 566.1 %reduce-scatter.33.cloned.1.call-start = ((), (), s32[]{:S(2)}) async-start(), calls=%async_computation.24 | async-start | bytes 2506752 | tf_op jit(solution)/shard_map/reduce_scatter | solution.py:317
  869.2 606.6 %all-reduce.46.cloned.1.call-start = ((), (), s32[]{:S(2)}) async-start(), calls=%async_computation.35 | async-start | bytes 165888 | tf_op jit(solution)/shard_map/psum | solution.py:292
  872.7 558.6 %copy-start.4 = (f32[2,128,768]{2,1,0:T(8,128)S(1)}, f32[2,128,768]{2,1,0:T(8,128)}, u32[]{:S(2)}) copy-start(f32[2,128,768]{2,1,0:T(8,128)} %copy-done.3) | copy-start | bytes 2359300
  872.9 558.4 %copy-start.19 = (bf16[2,128,768]{2,1,0:T(8,128)(2,1)S(1)}, bf16[2,128,768]{2,1,0:T(8,128)(2,1)}, u32[]{:S(2)}) copy-start(bf16[2,128,768]{2,1,0:T(8,128)(2,1)} %all-reduce.42.cloned.1.call-done) | copy-start | bytes 1179652
  1008.3 516.9 %all-reduce.48.cloned.1.call-start = ((), (), s32[]{:S(2)}) async-start(), calls=%async_computation.36 | async-start | bytes 1769472 | tf_op jit(solution)/shard_map/psum | solution.py:286
  (56 other events, 127.4 us)
Sparse Core Ops, SparseCore 0:
  10.8 47.1 all-gather.24
  176.2 21.9 all-reduce.27
  201.2 47.1 all-gather.26
  251.2 45.0 all-gather.28
  300.0 24.0 all-reduce.29
  326.1 46.5 all-gather.30
  459.4 22.1 all-reduce.31
  484.5 47.1 all-gather.32
  534.0 45.0 all-gather.34
  586.2 23.2 all-reduce.35
  612.5 26.1 all-reduce.33
  655.4 23.8 reduce-scatter.20
  681.8 22.1 reduce-scatter.22
  707.4 23.8 all-reduce.37
  739.0 25.3 all-reduce.39
  780.6 23.8 reduce-scatter.24
  806.9 22.0 reduce-scatter.26
  832.5 23.8 all-reduce.41
  860.1 73.2 reduce-scatter.38
  937.1 71.1 reduce-scatter.36
  1011.7 107.6 all-reduce.43
  1123.1 74.6 reduce-scatter.30
  1201.4 74.1 reduce-scatter.34
  1279.2 74.1 reduce-scatter.28
  1357.0 74.2 reduce-scatter.32
  1435.6 40.1 all-reduce.45
  1479.0 46.2 all-reduce.47
where the time goes:
time: 1540 us
  waiting for transfers between devices  913 us (59%)
  blocking collectives  373 us (24%)
  local copies, waits for them, and re-layouts  101 us (7%)
  matrix products  92.7 us (6%)
  other arithmetic  40.6 us (3%)
  between operations  17.3 us (1%)
    unnamed x30, waiting for transfers between devices  165 us
    reduce_scatter x2, waiting for transfers between devices, per_device(): lax.psum_scatter(grad_parts[5].astype(jnp.bfloat16), 'shard', scatter_dim...  156 us
    reduce_scatter x2, waiting for transfers between devices, per_device(): lax.psum_scatter(grad_parts[3].astype(jnp.bfloat16), 'shard', scatter_dim...  153 us
    all_gather x2, waiting for transfers between devices, per_device(): lax.all_gather(expansion[layer_index], 'shard', axis=0, tiled=True)  91.9 us
    all_gather x2, waiting for transfers between devices, per_device(): lax.all_gather(contraction[layer_index], 'shard', axis=1, tiled=True)  89.1 us
    unnamed x1, blocking collectives  75.6 us
    reduce_scatter x2, waiting for transfers between devices, per_device(): lax.psum_scatter(value_full.astype(jnp.bfloat16), 'context', scatter_dime...  49.3 us
    all_gather x2, blocking collectives, per_device(): lax.all_gather(offsets[layer_index], 'shard', axis=1, tiled=True)  48.7 us
  transfers between devices with their start and end apart: 27, of which 20 were waited for; matrix products, arithmetic and copies ran while one was open for 9% of the time, Pallas kernels for 0%

commit v1 on v0

--- a/solution.py
+++ b/solution.py
@@ -213,7 +213,9 @@
         feed_partial = jnp.einsum(
             "rtf,df->rtd", hidden_half, up_weight, preferred_element_type=jnp.float32
         )
-        feed_back = lax.psum(feed_partial.astype(jnp.bfloat16), "tensor").astype(jnp.float32)
+        feed_back = jnp.sum(
+            lax.all_gather(feed_partial.astype(jnp.bfloat16), "tensor"), axis=0
+        ).astype(jnp.float32)
         gain_two = jnp.sum(feed_back * normed_two, axis=(0, 1))
         offset_two = jnp.sum(feed_back, axis=(0, 1))
         middle_back = upstream + norm_backward(feed_back, normed_two, spread_two, gain_float[1])

time: 1540 us -> 1490 us (0.968)
  waiting for transfers between devices: 913 us -> 856 us
    psum x2 -> x0, waiting for transfers between devices: 44.5 us -> none  [per_device(): lax.psum(feed_partial.astype(jnp.bfloat16), 'tensor').astype(jnp.float32)]
    unnamed x30 -> x28, waiting for transfers between devices: 165 us -> 165 us
  transfers between devices with their start and end apart: 27 -> 25, of which waited for: 20 -> 18; matrix products, arithmetic and copies ran while one was open for 9% -> 9% of each run, Pallas kernels for 0% -> 0%
where the time goes in v1:
time: 1490 us; the launch traced here: 1480 us
  waiting for transfers between devices  856 us (57%)
  blocking collectives  377 us (25%)
  local copies, waits for them, and re-layouts  96.9 us (7%)
  matrix products  91.8 us (6%)
  other arithmetic  44 us (3%)
  between operations  17.1 us (1%)
    unnamed x28, waiting for transfers between devices  165 us
    reduce_scatter x2, waiting for transfers between devices, per_device(): lax.psum_scatter(grad_parts[5].astype(jnp.bfloat16), 'shard', scatter_dim...  156 us
    reduce_scatter x2, waiting for transfers between devices, per_device(): lax.psum_scatter(grad_parts[3].astype(jnp.bfloat16), 'shard', scatter_dim...  153 us
    all_gather x2, waiting for transfers between devices, per_device(): lax.all_gather(expansion[layer_index], 'shard', axis=0, tiled=True)  93.6 us
    all_gather x2, waiting for transfers between devices, per_device(): lax.all_gather(contraction[layer_index], 'shard', axis=1, tiled=True)  89.1 us
    unnamed x1, blocking collectives  75.5 us
    reduce_scatter x2, waiting for transfers between devices, per_device(): lax.psum_scatter(value_full.astype(jnp.bfloat16), 'context', scatter_dime...  49.1 us
    all_gather x2, blocking collectives, per_device(): lax.all_gather(offsets[layer_index], 'shard', axis=1, tiled=True)  48.7 us
  transfers between devices with their start and end apart: 25, of which 18 were waited for; matrix products, arithmetic and copies ran while one was open for 9% of the time, Pallas kernels for 0%

profile of v1, /device:TPU:0, one launch (start us, length us, event | category | flops | bytes accessed | tf_op | source)
XLA Modules:
  0.0 1483.9 jit_solution(17113137418452583356)
XLA Ops:
  10.4 25.5 %all-gather.1 = bf16[1,4,768]{1,0,2:T(2,128)(2,1)S(1)} all-gather(bf16[1,4,48]{1,0,2:T(2,128)(2,1)S(1)} %copy.288), channel_id=3, replica_groups=mesh['shard'=16,'context'=4,'tensor'=2] {'shard'}, dimensions={2}, use_global_device_ids=true | all-gather | bytes 6528 | tf_op jit(solution)/shard_map/all_gather | solution.py:79
  37.0 23.4 %all-gather = bf16[1,2,768]{1,0,2:T(2,128)(2,1)S(1)} all-gather(bf16[1,2,48]{1,0,2:T(2,128)(2,1)S(1)} %copy.287), channel_id=2, replica_groups=mesh['shard'=16,'context'=4,'tensor'=2] {'shard'}, dimensions={2}, use_global_device_ids=true | all-gather | bytes 3264 | tf_op jit(solution)/shard_map/all_gather | solution.py:78
  61.4 21.3 %all-gather.3 = bf16[1,2,6,64]{2,1,0,3:T(2,128)(2,1)S(1)} all-gather(bf16[1,2,6,4]{2,1,0,3:T(2,128)(2,1)S(1)} %copy.289), channel_id=5, replica_groups=mesh['shard'=16,'context'=4,'tensor'=2] {'shard'}, dimensions={3}, use_global_device_ids=true | all-gather | bytes 1632 | tf_op jit(solution)/shard_map/all_gather | solution.py:73
  83.1 10.0 all_gather.91
  93.1 23.9 %all-gather.5 = bf16[1,384,768]{1,2,0:T(8,128)(2,1)S(1)} all-gather(bf16[1,384,48]{1,2,0:T(8,128)(2,1)S(1)} %get-tuple-element.105), channel_id=7, replica_groups=mesh['shard'=16,'context'=4,'tensor'=2] {'shard'}, dimensions={2}, use_global_device_ids=true | all-gather | bytes 626688 | tf_op jit(solution)/shard_map/all_gather | solution.py:74
  117.2 4.6 slice_reduce_fusion.8
  122.1 11.0 slice_reduce_fusion.6
  136.3 14.4 all-gather.4
  157.9 13.3 all_gather.90
  171.6 3.1 convolution_convert_fusion.5
  178.3 21.3 %all-gather.7 = bf16[1,24,64]{1,0,2:T(2,128)(2,1)S(1)} all-gather(bf16[1,24,4]{1,0,2:T(2,128)(2,1)S(1)} %copy.290), channel_id=9, replica_groups=mesh['shard'=16,'context'=4,'tensor'=2] {'shard'}, dimensions={2}, use_global_device_ids=true | all-gather | bytes 3264 | tf_op jit(solution)/shard_map/all_gather | solution.py:76
  201.3 47.0 %all-gather.29.cloned.1.call-done = bf16[1,768,1536]{2,1,0:T(8,128)(2,1)} async-done(((bf16[1,48,1536]{2,1,0:T(8,128)(2,1)}), bf16[1,768,1536]{2,1,0:T(8,128)(2,1)}) %all-gather.29.cloned.1.call-update) | async-done | bytes 2359312 | tf_op jit(solution)/shard_map/all_gather | solution.py:75
  248.4 2.5 convolution_add_fusion.1
  250.9 45.3 %all-gather.31.cloned.1.call-done = bf16[1,1536,768]{1,2,0:T(8,128)(2,1)} async-done(((bf16[1,1536,48]{1,2,0:T(8,128)(2,1)}), bf16[1,1536,768]{1,2,0:T(8,128)(2,1)}) %all-gather.31.cloned.1.call-update) | async-done | bytes 2359312 | tf_op jit(solution)/shard_map/all_gather | solution.py:77
  296.3 3.6 fusion.6
  300.7 23.3 %all-gather.10 = bf16[1,4,768]{1,0,2:T(2,128)(2,1)S(1)} all-gather(bf16[1,4,48]{1,0,2:T(2,128)(2,1)S(1)} %copy.292), channel_id=12, replica_groups=mesh['shard'=16,'context'=4,'tensor'=2] {'shard'}, dimensions={2}, use_global_device_ids=true | all-gather | bytes 6528 | tf_op jit(solution)/shard_map/all_gather | solution.py:79
  324.5 22.4 %all-gather.9 = bf16[1,2,768]{1,0,2:T(2,128)(2,1)S(1)} all-gather(bf16[1,2,48]{1,0,2:T(2,128)(2,1)S(1)} %copy.291), channel_id=11, replica_groups=mesh['shard'=16,'context'=4,'tensor'=2] {'shard'}, dimensions={2}, use_global_device_ids=true | all-gather | bytes 3264 | tf_op jit(solution)/shard_map/all_gather | solution.py:78
  347.3 22.1 %all-gather.12 = bf16[1,2,6,64]{2,1,0,3:T(2,128)(2,1)S(1)} all-gather(bf16[1,2,6,4]{2,1,0,3:T(2,128)(2,1)S(1)} %copy.293), channel_id=14, replica_groups=mesh['shard'=16,'context'=4,'tensor'=2] {'shard'}, dimensions={3}, use_global_device_ids=true | all-gather | bytes 1632 | tf_op jit(solution)/shard_map/all_gather | solution.py:73
  370.8 24.5 %all-gather.14 = bf16[1,384,768]{1,2,0:T(8,128)(2,1)} all-gather(bf16[1,384,48]{1,2,0:T(8,128)(2,1)S(1)} %get-tuple-element.104), channel_id=16, replica_groups=mesh['shard'=16,'context'=4,'tensor'=2] {'shard'}, dimensions={2}, use_global_device_ids=true | all-gather | bytes 626688 | tf_op jit(solution)/shard_map/all_gather | solution.py:74
  395.4 4.6 slice_reduce_fusion.2
  399.9 11.2 slice_reduce_fusion
  416.2 15.3 %all-gather.13 = bf16[1,2,512,384]{3,2,0,1:T(8,128)(2,1)} all-gather(bf16[1,2,128,384]{3,2,0,1:T(8,128)(2,1)S(1)} %slice.234), channel_id=15, replica_groups=mesh['shard'=16,'context'=4,'tensor'=2] {'context'}, dimensions={2}, use_global_device_ids=true | all-gather | bytes 983040 | tf_op jit(solution)/shard_map/all_gather | solution.py:103
  438.6 13.3 all_gather.101
  453.0 3.1 convolution_convert_fusion.4
  459.7 22.5 %all-gather.16 = bf16[1,24,64]{1,0,2:T(2,128)(2,1)S(1)} all-gather(bf16[1,24,4]{1,0,2:T(2,128)(2,1)S(1)} %copy.294), channel_id=18, replica_groups=mesh['shard'=16,'context'=4,'tensor'=2] {'shard'}, dimensions={2}, use_global_device_ids=true | all-gather | bytes 3264 | tf_op jit(solution)/shard_map/all_gather | solution.py:76
  484.0 46.6 %all-gather.35.cloned.1.call-done = bf16[1,768,1536]{2,1,0:T(8,128)(2,1)} async-done(((bf16[1,48,1536]{2,1,0:T(8,128)(2,1)}), bf16[1,768,1536]{2,1,0:T(8,128)(2,1)}) %all-gather.35.cloned.1.call-update) | async-done | bytes 2359312 | tf_op jit(solution)/shard_map/all_gather | solution.py:75
  530.6 3.7 convolution_add_fusion
  534.3 43.8 %all-gather.37.cloned.1.call-done = bf16[1,1536,768]{1,2,0:T(8,128)(2,1)} async-done(((bf16[1,1536,48]{1,2,0:T(8,128)(2,1)}), bf16[1,1536,768]{1,2,0:T(8,128)(2,1)}) %all-gather.37.cloned.1.call-update) | async-done | bytes 2359312 | tf_op jit(solution)/shard_map/all_gather | solution.py:77
  578.0 4.1 fusion.3
  582.2 4.5 fusion.157
  587.5 2.7 all-gather.18
  593.7 12.6 all-reduce.32.cloned.1.call-done
  606.3 3.3 fusion.140
  614.4 3.5 multiply_convert_fusion.1
  622.7 3.8 convolution_convert_fusion.2
  628.9 2.9 fusion.146
  632.0 14.6 reduce-scatter.21.cloned.1.call-done
  646.6 24.5 %reduce-scatter.23.cloned.1.call-done = bf16[2,128,384]{2,1,0:T(8,128)(2,1)} async-done(((bf16[2,512,384]{2,1,0:T(8,128)(2,1)}), bf16[2,128,384]{2,1,0:T(8,128)(2,1)}) %reduce-scatter.23.cloned.1.call-update) | async-done | bytes 196624 | tf_op jit(solution)/shard_map/reduce_scatter | solution.py:257
  671.1 3.2 fusion.50
  674.4 23.9 %all-reduce.34.cloned.1.call-done = bf16[2,128,768]{2,1,0:T(8,128)(2,1)} async-done(((bf16[2,128,768]{2,1,0:T(8,128)(2,1)}), bf16[2,128,768]{2,1,0:T(8,128)(2,1)}) %all-reduce.34.cloned.1.call-update) | async-done | bytes 393232 | tf_op jit(solution)/shard_map/psum | solution.py:271
  705.3 2.5 all-gather.19
  717.6 3.5 multiply_convert_fusion
  726.2 3.9 convolution_convert_fusion
  730.1 2.4 copy.239
  732.6 3.0 fusion.145
  737.4 12.6 reduce-scatter.25.cloned.1.call-done
  750.0 24.6 %reduce-scatter.27.cloned.1.call-done = bf16[2,128,384]{2,1,0:T(8,128)(2,1)} async-done(((bf16[2,512,384]{2,1,0:T(8,128)(2,1)}), bf16[2,128,384]{2,1,0:T(8,128)(2,1)}) %reduce-scatter.27.cloned.1.call-update) | async-done | bytes 196624 | tf_op jit(solution)/shard_map/reduce_scatter | solution.py:257
  774.6 3.3 fusion.53
  777.9 2.5 fusion.43
  782.9 3.1 fusion.35
  786.0 5.3 copy.244
  793.4 5.2 copy.242
  803.2 3.9 bitcast_convert_fusion
  808.2 2.4 bitcast_convert_fusion.3
  812.2 2.4 bitcast_convert_fusion.1
  821.2 75.5 %all-reduce.12 = (bf16[2,6,64]{1,0,2:T(2,128)(2,1)S(1)}, bf16[2,6,64]{1,0,2:T(2,128)(2,1)S(1)}, bf16[24,64]{1,0:T(8,128)(2,1)S(1)}, bf16[24,64]{1,0:T(8,128)(2,1...) all-reduce(bf16[2,6,64]{1,0,2:T(2,128)(2,1)S(1)} %copy.249, ...), channel_id=29, replica_groups=mesh['shard'=16,'context'=4,'tensor'=2] {'shard'}, use_global_device_ids=true, to_apply=%region_44.45.clone | all-reduce | flops 13824 | bytes 55296
  901.9 51.6 %reduce-scatter.37.cloned.1.call-done = bf16[384,48]{0,1:T(8,128)(2,1)} async-done(((bf16[384,768]{0,1:T(8,128)(2,1)}), bf16[384,48]{0,1:T(8,128)(2,1)}) %reduce-scatter.37.cloned.1.call-update) | async-done | bytes 36880
  953.6 111.1 %all-reduce.38.cloned.1.call-done = (bf16[3,768,384]{2,0,1:T(4,128)(2,1)}, bf16[3,768,384]{2,0,1:T(4,128)(2,1)}) async-done(((bf16[3,768,384]{2,0,1:T(4,128)(2,1)}, bf16[3,768,384]{2,0,1:T(4,128)(2,1)}), (bf16[3,768,384]{2,0,1:T(4,128)(2,1)}, bf16[3,768,384]{2,0,1:T(4,128)(2,1)})) %all-reduce.38.cloned.1.call-update) | async-done | bytes 3538960
  1067.9 75.0 %reduce-scatter.31.cloned.1.call-done = bf16[48,1536]{1,0:T(8,128)(2,1)} async-done(((bf16[768,1536]{1,0:T(8,128)(2,1)}), bf16[48,1536]{1,0:T(8,128)(2,1)}) %reduce-scatter.31.cloned.1.call-update) | async-done | bytes 147472 | tf_op jit(solution)/shard_map/reduce_scatter | solution.py:307
  1142.9 78.0 %reduce-scatter.35.cloned.1.call-done = bf16[1536,48]{0,1:T(8,128)(2,1)} async-done(((bf16[1536,768]{0,1:T(8,128)(2,1)}), bf16[1536,48]{0,1:T(8,128)(2,1)}) %reduce-scatter.35.cloned.1.call-update) | async-done | bytes 147472 | tf_op jit(solution)/shard_map/reduce_scatter | solution.py:319
  1220.9 77.9 %reduce-scatter.29.cloned.1.call-done = bf16[48,1536]{1,0:T(8,128)(2,1)} async-done(((bf16[768,1536]{1,0:T(8,128)(2,1)}), bf16[48,1536]{1,0:T(8,128)(2,1)}) %reduce-scatter.29.cloned.1.call-update) | async-done | bytes 147472 | tf_op jit(solution)/shard_map/reduce_scatter | solution.py:307
  1298.8 77.8 %reduce-scatter.33.cloned.1.call-done = bf16[1536,48]{0,1:T(8,128)(2,1)} async-done(((bf16[1536,768]{0,1:T(8,128)(2,1)}), bf16[1536,48]{0,1:T(8,128)(2,1)}) %reduce-scatter.33.cloned.1.call-update) | async-done | bytes 147472 | tf_op jit(solution)/shard_map/reduce_scatter | solution.py:319
  1377.8 43.4 %all-reduce.40.cloned.1.call-done = (bf16[1,2,6,4]{2,3,1,0:T(4,128)(2,1)}, bf16[1,2,6,4]{2,3,1,0:T(4,128)(2,1)}, bf16[1,384,48]{1,2,0:T(8,128)(2,1)}, bf16[1,384...) async-done(((bf16[1,2,6,4]{2,3,1,0:T(4,128)(2,1)}, ...) | async-done | bytes 75472 | tf_op jit(solution)/shard_map/psum | solution.py:294
  1427.8 43.0 %all-reduce.42.cloned.1.call-done = (bf16[1,3,48,384]{3,1,2,0:T(4,128)(2,1)}, bf16[1,3,48,384]{3,1,2,0:T(4,128)(2,1)}, bf16[1,48,1536]{2,1,0:T(8,128)(2,1)}, bf1...) async-done(((bf16[1,3,48,384]{3,1,2,0:T(4,128)(2,1)}, bf16[1,3,48,384]{3,1,2,0:T(4,128)(2,1)}, bf16[1,48,1536]{2,1,0:T(8,128)(2,1)}, ...) | async-done | bytes 811024 | tf_op jit(solution)/shard_map/psum | solution.py:288
  (437 shorter events, 123.0 us)
Async XLA Ops:
  7.2 29.1 %copy-start.98 = (bf16[2,2,48]{2,1,0:T(2,128)(2,1)S(1)}, bf16[2,2,48]{2,1,0:T(2,128)(2,1)}, u32[]{:S(2)}) copy-start(bf16[2,2,48]{2,1,0:T(2,128)(2,1)} %param.19) | copy-start | bytes 1156
  7.2 53.6 %copy-start.103 = (s32[2,128]{1,0:T(2,128)S(1)}, s32[2,128]{1,0:T(2,128)}, u32[]{:S(2)}) copy-start(s32[2,128]{1,0:T(2,128)} %param.12) | copy-start | bytes 3076
  7.2 53.6 %copy-start.91 = (bf16[2,2,6,4]{2,3,1,0:T(4,128)(2,1)S(1)}, bf16[2,2,6,4]{2,3,1,0:T(4,128)(2,1)}, u32[]{:S(2)}) copy-start(bf16[2,2,6,4]{2,3,1,0:T(4,128)(2,1)} %param.14) | copy-start | bytes 580
  7.2 75.7 %copy-start = (f32[2,128,768]{2,1,0:T(8,128)S(1)}, f32[2,128,768]{2,1,0:T(8,128)}, u32[]{:S(2)}) copy-start(f32[2,128,768]{2,1,0:T(8,128)} %param.11) | copy-start | bytes 2359300
  7.2 126.0 %all-gather.27.cloned.1.call-start = ((), (), s32[]{:S(2)}) async-start(), calls=%async_computation.24 | async-start | bytes 1880064 | tf_op jit(solution)/shard_map/all_gather | solution.py:72
  9.0 84.1 %copy-start.46 = (bf16[2,384,48]{1,2,0:T(8,128)(2,1)S(1)}, bf16[2,384,48]{1,2,0:T(8,128)(2,1)}, u32[]{:S(2)}) copy-start(bf16[2,384,48]{1,2,0:T(8,128)(2,1)} %param.15) | copy-start | bytes 221188
  9.0 190.7 %all-reduce.26.cloned.1.call-start = ((), (), s32[]{:S(2)}) async-start(), calls=%async_computation.10 | async-start | bytes 1572864 | tf_op jit(solution)/shard_map/psum | solution.py:128
  82.8 71.6 %copy-start.56 = (f32[6,64]{1,0:T(8,128)}, f32[6,64]{1,0:T(8,128)S(1)}, u32[]{:S(2)}) copy-start(f32[6,64]{1,0:T(8,128)S(1)} %copy.213) | copy-start | bytes 4612
  117.0 57.7 %copy-start.12 = (bf16[1,384,768]{1,2,0:T(8,128)(2,1)}, bf16[1,384,768]{1,2,0:T(8,128)(2,1)S(1)}, u32[]{:S(2)}) copy-start(bf16[1,384,768]{1,2,0:T(8,128)(2,1)S(1)} %all-gather.5) | copy-start | bytes 1769476
  117.0 18.5 %copy-start.51 = (f32[2,128]{1,0:T(2,128)}, f32[2,128]{1,0:T(2,128)S(1)}, u32[]{:S(2)}) copy-start(f32[2,128]{1,0:T(2,128)S(1)} %broadcast_multiply_fusion.11) | copy-start | bytes 3076
  121.8 13.7 copy-start.59
  122.1 49.4 %copy-start.22 = (pred[2,128,512]{2,1,0:T(8,128)(4,1)}, pred[2,128,512]{2,1,0:T(8,128)(4,1)S(1)}, u32[]{:S(2)}) copy-start(pred[2,128,512]{2,1,0:T(8,128)(4,1)S(1)} %compare_and_fusion) | copy-start | bytes 393220
  133.2 115.2 %copy-start.68 = (f32[768]{0:T(1024)}, f32[768]{0:T(1024)S(1)}, u32[]{:S(2)}) copy-start(f32[768]{0:T(1024)S(1)} %get-tuple-element.49) | copy-start | bytes 9220
  157.9 13.7 copy-start.85
  176.1 72.3 %all-gather.29.cloned.1.call-start = ((), (), s32[]{:S(2)}) async-start(), calls=%async_computation.25 | async-start | bytes 2506752 | tf_op jit(solution)/shard_map/all_gather | solution.py:75
  176.9 119.4 %all-gather.31.cloned.1.call-start = ((), (), s32[]{:S(2)}) async-start(), calls=%async_computation.26 | async-start | bytes 2506752 | tf_op jit(solution)/shard_map/all_gather | solution.py:77
  177.7 233.5 %all-reduce.28.cloned.1.call-start = ((), (), s32[]{:S(2)}) async-start(), calls=%async_computation.11 | async-start | bytes 1572864 | tf_op jit(solution)/shard_map/psum | solution.py:138
  201.1 49.8 %copy-start.61 = (f32[2,128]{1,0:T(2,128)}, f32[2,128]{1,0:T(2,128)S(1)}, u32[]{:S(2)}) copy-start(f32[2,128]{1,0:T(2,128)S(1)} %broadcast_multiply_fusion.10) | copy-start | bytes 3076
  201.3 49.6 %copy-start.73 = (f32[2,128]{1,0:T(2,128)}, f32[2,128]{1,0:T(2,128)S(1)}, u32[]{:S(2)}) copy-start(f32[2,128]{1,0:T(2,128)S(1)} %add_rsqrt_fusion.2) | copy-start | bytes 3076
  250.9 45.3 %copy-start.105 = (f32[2,128,1536]{2,1,0:T(8,128)}, f32[2,128,1536]{2,1,0:T(8,128)S(1)}, u32[]{:S(2)}) copy-start(f32[2,128,1536]{2,1,0:T(8,128)S(1)} %convolution_add_fusion.1) | copy-start | bytes 4718596
  250.9 49.6 %copy-start.94 = (bf16[1,4,48]{2,1,0:T(4,128)(2,1)S(1)}, bf16[1,4,48]{2,1,0:T(4,128)(2,1)}, u32[]{:S(2)}) copy-start(bf16[1,4,48]{2,1,0:T(4,128)(2,1)} %get-tuple-element.115) | copy-start | bytes 1156
  299.9 24.5 %copy-start.97 = (bf16[1,2,48]{2,1,0:T(2,128)(2,1)S(1)}, bf16[1,2,48]{2,1,0:T(2,128)(2,1)}, u32[]{:S(2)}) copy-start(bf16[1,2,48]{2,1,0:T(2,128)(2,1)} %get-tuple-element.116) | copy-start | bytes 580
  299.9 47.4 %copy-start.89 = (bf16[1,2,6,4]{2,3,1,0:T(4,128)(2,1)S(1)}, bf16[1,2,6,4]{2,3,1,0:T(4,128)(2,1)}, u32[]{:S(2)}) copy-start(bf16[1,2,6,4]{2,3,1,0:T(4,128)(2,1)} %get-tuple-element.110) | copy-start | bytes 292
  299.9 112.8 %all-gather.33.cloned.1.call-start = ((), (), s32[]{:S(2)}) async-start(), calls=%async_computation.27 | async-start | bytes 1880064 | tf_op jit(solution)/shard_map/all_gather | solution.py:72
  300.5 181.9 %all-reduce.30.cloned.1.call-start = ((), (), s32[]{:S(2)}) async-start(), calls=%async_computation.12 | async-start | bytes 1572864 | tf_op jit(solution)/shard_map/psum | solution.py:128
  437.3 15.7 %copy-start.24 = (pred[2,128,512]{2,1,0:T(8,128)(4,1)S(1)}, pred[2,128,512]{2,1,0:T(8,128)(4,1)}, u32[]{:S(2)}) copy-start(pred[2,128,512]{2,1,0:T(8,128)(4,1)} %copy-done.22) | copy-start | bytes 393220
  437.3 18.9 %copy-start.87 = (f32[2,6,128]{2,1,0:T(8,128)}, f32[2,6,128]{2,1,0:T(8,128)S(1)}, u32[]{:S(2)}) copy-start(f32[2,6,128]{2,1,0:T(8,128)S(1)} %log_add_fusion) | copy-start | bytes 18436
  456.2 26.2 %copy-start.72 = (f32[768]{0:T(1024)S(1)}, f32[768]{0:T(1024)}, u32[]{:S(2)}) copy-start(f32[768]{0:T(1024)} %get-tuple-element.44) | copy-start | bytes 9220
  458.2 72.4 %all-gather.35.cloned.1.call-start = ((), (), s32[]{:S(2)}) async-start(), calls=%async_computation.28 | async-start | bytes 2506752 | tf_op jit(solution)/shard_map/all_gather | solution.py:75
  458.2 72.3 %copy-start.70 = (f32[768]{0:T(1024)S(1)}, f32[768]{0:T(1024)}, u32[]{:S(2)}) copy-start(f32[768]{0:T(1024)} %get-tuple-element.43) | copy-start | bytes 9220
  458.9 119.1 %all-gather.37.cloned.1.call-start = ((), (), s32[]{:S(2)}) async-start(), calls=%async_computation.29 | async-start | bytes 2506752 | tf_op jit(solution)/shard_map/all_gather | solution.py:77
  459.7 146.7 %all-reduce.32.cloned.1.call-start = ((), (), s32[]{:S(2)}) async-start(), calls=%async_computation.13 | async-start | bytes 1572864 | tf_op jit(solution)/shard_map/psum | solution.py:138
  483.7 50.5 %copy-start.66 = (f32[2,128]{1,0:T(2,128)}, f32[2,128]{1,0:T(2,128)S(1)}, u32[]{:S(2)}) copy-start(f32[2,128]{1,0:T(2,128)S(1)} %broadcast_multiply_fusion.8) | copy-start | bytes 3076
  484.0 50.3 %copy-start.75 = (f32[2,128]{1,0:T(2,128)}, f32[2,128]{1,0:T(2,128)S(1)}, u32[]{:S(2)}) copy-start(f32[2,128]{1,0:T(2,128)S(1)} %add_rsqrt_fusion) | copy-start | bytes 3076
  582.1 64.5 %reduce-scatter.21.cloned.1.call-start = ((), (), s32[]{:S(2)}) async-start(), calls=%async_computation.14 | async-start | bytes 983040 | tf_op jit(solution)/shard_map/reduce_scatter | solution.py:254
  609.6 4.7 copy-start.25
  609.6 4.7 copy-start.88
  622.7 48.5 %reduce-scatter.23.cloned.1.call-start = ((), (), s32[]{:S(2)}) async-start(), calls=%async_computation.15 | async-start | bytes 983040 | tf_op jit(solution)/shard_map/reduce_scatter | solution.py:257
  628.8 69.4 %all-reduce.34.cloned.1.call-start = ((), (), s32[]{:S(2)}) async-start(), calls=%async_computation.16 | async-start | bytes 786432 | tf_op jit(solution)/shard_map/psum | solution.py:271
  632.0 42.3 %copy-start.44 = (bf16[1,2,128,384]{3,2,0,1:T(8,128)(2,1)}, bf16[1,2,128,384]{3,2,0,1:T(8,128)(2,1)S(1)}, u32[]{:S(2)}) copy-start(bf16[1,2,128,384]{3,2,0,1:T(8,128)(2,1)S(1)} %copy.236) | copy-start | bytes 589828
  671.1 27.1 %copy-start.54 = (f32[2,128]{1,0:T(2,128)S(1)}, f32[2,128]{1,0:T(2,128)}, u32[]{:S(2)}) copy-start(f32[2,128]{1,0:T(2,128)} %copy-done.53) | copy-start | bytes 3076
  671.1 27.1 %copy-start.64 = (f32[2,128]{1,0:T(2,128)S(1)}, f32[2,128]{1,0:T(2,128)}, u32[]{:S(2)}) copy-start(f32[2,128]{1,0:T(2,128)} %copy-done.63) | copy-start | bytes 3076
  674.3 75.6 %reduce-scatter.25.cloned.1.call-start = ((), (), s32[]{:S(2)}) async-start(), calls=%async_computation.17 | async-start | bytes 983040 | tf_op jit(solution)/shard_map/reduce_scatter | solution.py:254
  717.6 4.7 copy-start.18
  717.6 4.7 copy-start.57
  726.0 48.6 %reduce-scatter.27.cloned.1.call-start = ((), (), s32[]{:S(2)}) async-start(), calls=%async_computation.18 | async-start | bytes 983040 | tf_op jit(solution)/shard_map/reduce_scatter | solution.py:257
  732.5 86.0 %all-reduce.36.cloned.1.call-start = ((), (), s32[]{:S(2)}) async-start(), calls=%async_computation.19 | async-start | bytes 786432 | tf_op jit(solution)/shard_map/psum | solution.py:271
  777.8 124.1 %reduce-scatter.39.cloned.1.call-start = ((), (), s32[]{:S(2)}) async-start(), calls=%async_computation.31 | async-start | bytes 626688
  780.4 173.1 %reduce-scatter.37.cloned.1.call-start = ((), (), s32[]{:S(2)}) async-start(), calls=%async_computation.30 | async-start | bytes 626688
  782.8 281.8 %all-reduce.38.cloned.1.call-start = ((), (), s32[]{:S(2)}) async-start(), calls=%async_computation.32 | async-start | bytes 9437184
  786.0 5.3 copy-start.43
  786.0 5.3 copy-start.45
  786.0 5.3 copy-start.48
  786.0 5.3 copy-start.52
  786.0 5.3 copy-start.60
  786.0 5.3 copy-start.102
  798.6 344.3 %reduce-scatter.31.cloned.1.call-start = ((), (), s32[]{:S(2)}) async-start(), calls=%async_computation.21 | async-start | bytes 2506752 | tf_op jit(solution)/shard_map/reduce_scatter | solution.py:307
  802.1 418.8 %reduce-scatter.35.cloned.1.call-start = ((), (), s32[]{:S(2)}) async-start(), calls=%async_computation.23 | async-start | bytes 2506752 | tf_op jit(solution)/shard_map/reduce_scatter | solution.py:319
  807.1 491.7 %reduce-scatter.29.cloned.1.call-start = ((), (), s32[]{:S(2)}) async-start(), calls=%async_computation.20 | async-start | bytes 2506752 | tf_op jit(solution)/shard_map/reduce_scatter | solution.py:307
  810.6 566.0 %reduce-scatter.33.cloned.1.call-start = ((), (), s32[]{:S(2)}) async-start(), calls=%async_computation.22 | async-start | bytes 2506752 | tf_op jit(solution)/shard_map/reduce_scatter | solution.py:319
  814.8 606.4 %all-reduce.40.cloned.1.call-start = ((), (), s32[]{:S(2)}) async-start(), calls=%async_computation.33 | async-start | bytes 165888 | tf_op jit(solution)/shard_map/psum | solution.py:294
  818.3 558.3 %copy-start.4 = (f32[2,128,768]{2,1,0:T(8,128)S(1)}, f32[2,128,768]{2,1,0:T(8,128)}, u32[]{:S(2)}) copy-start(f32[2,128,768]{2,1,0:T(8,128)} %copy-done.3) | copy-start | bytes 2359300
  818.6 558.1 %copy-start.21 = (bf16[2,128,768]{2,1,0:T(8,128)(2,1)S(1)}, bf16[2,128,768]{2,1,0:T(8,128)(2,1)}, u32[]{:S(2)}) copy-start(bf16[2,128,768]{2,1,0:T(8,128)(2,1)} %all-reduce.36.cloned.1.call-done) | copy-start | bytes 1179652
  953.5 517.3 %all-reduce.42.cloned.1.call-start = ((), (), s32[]{:S(2)}) async-start(), calls=%async_computation.34 | async-start | bytes 1769472 | tf_op jit(solution)/shard_map/psum | solution.py:288
  (69 other events, 173.2 us)
Sparse Core Ops, SparseCore 0:
  10.8 47.1 all-gather.26
  176.2 21.9 all-reduce.25
  201.2 47.1 all-gather.28
  251.2 45.0 all-gather.30
  300.0 24.0 all-reduce.27
  326.1 46.5 all-gather.32
  458.3 22.0 all-reduce.29
  483.4 47.1 all-gather.34
  532.9 45.0 all-gather.36
  582.3 24.0 all-reduce.31
  622.8 23.7 reduce-scatter.20
  648.9 22.2 reduce-scatter.22
  674.5 23.7 all-reduce.33
  726.1 23.8 reduce-scatter.24
  752.3 22.1 reduce-scatter.26
  777.9 23.7 all-reduce.35
  805.3 73.3 reduce-scatter.38
  882.3 71.1 reduce-scatter.36
  956.9 107.6 all-reduce.37
  1068.2 74.6 reduce-scatter.30
  1146.6 74.2 reduce-scatter.34
  1224.6 74.1 reduce-scatter.28
  1302.5 74.1 reduce-scatter.32
  1381.0 40.2 all-reduce.39
  1424.5 46.2 all-reduce.41
